TPU v7x, 32 devices: a whole 2x2x4 slice. The times are simulated.
32 devices in a mesh: chan: 4 (over y, x), slab: 8 (over z, core).
Axes of the slice: x: 2, y: 2, z: 4, core: 2. Of those that a mesh axis runs over, the one named last changes fastest.
Arguments:
- volume: bfloat16 [128, 16, 128, 128], P('chan', 'slab'), may hold values from -6 to 6
- weight_one: bfloat16 [3, 3, 3, 128, 256], P(None, None, None, 'chan'), may hold values from -0.125 to 0.125
- bias_one: float32 [256], replicated, may hold values from -3 to 3
- weight_two: bfloat16 [3, 3, 3, 32, 256], replicated, may hold values from -0.21875 to 0.21875
- bias_two: float32 [256], replicated, may hold values from -3 to 3
Outputs:
- activated: bfloat16 [8, 64, 64, 256], P('slab', 'chan')
- grouped: bfloat16 [8, 64, 64, 256], P('slab', 'chan')
All inputs are finite; a program needn't handle non-finite values.
Results may differ from a plain program's by a relative error of at most 0.018.
Values may be sent and summed in bfloat16 or wider, within the bound.
A program may use at most 64 MiB of HBM per device.

v0:
```python
import jax
import jax.numpy as jnp
from jax import lax
from jax.sharding import PartitionSpec as P


def shifted(block, axis, distance):
    devices = range(lax.axis_size(axis))
    route = [(i - distance, i) for i in devices if i - distance in devices]
    return lax.ppermute(block, axis, route)


def with_halo(cells, sides, width):
    for axis, dim in sides:
        count = lax.axis_size(axis)
        ends = count - 1
        head = lax.slice_in_dim(cells, 0, width, axis=dim)
        tail = lax.slice_in_dim(cells, cells.shape[dim] - width, cells.shape[dim], axis=dim)
        cells = jnp.concatenate(
            [
                lax.ppermute(tail, axis, [(i, (i + 1) % count) for i in range(ends)]),
                cells,
                lax.ppermute(head, axis, [((i + 1) % count, i) for i in range(ends)]),
            ],
            axis=dim,
        )
    return cells


def leaky(value):
    return jnp.where(value > 0, value, 0.3 * value)


def strided_conv(source, kernel, padding, out_spec):
    result = lax.conv_general_dilated(
        source[None],
        kernel,
        (2, 2, 2),
        padding,
        dimension_numbers=("NCDHW", "DHWIO", out_spec),
        preferred_element_type=jnp.float32,
    )[0]
    rounded = lax.optimization_barrier(result.astype(jnp.bfloat16))
    return rounded.astype(jnp.float32)


def local(volume, weight_one, bias_one, weight_two, bias_two):
    planes = volume.shape[1]
    width_out = weight_one.shape[4]
    parts = lax.axis_size("chan")
    lower = shifted(volume[:, planes - 1 :], "slab", 1)
    extended = jnp.concatenate([lower, volume], axis=1)
    partial_sum = strided_conv(extended, weight_one, ((0, 0), (1, 0), (1, 0)), "NDHWC")
    summed = lax.psum_scatter(
        partial_sum.astype(jnp.bfloat16), "chan", scatter_dimension=3, tiled=True
    ).astype(jnp.float32)
    share = width_out // parts
    bias_here = lax.dynamic_slice_in_dim(bias_one, lax.axis_index("chan") * share, share)
    act_part = leaky(summed + bias_here).astype(jnp.bfloat16)
    activated = lax.all_to_all(act_part, "chan", split_axis=1, concat_axis=3, tiled=True)
    padded = with_halo(activated, (("chan", 1), ("slab", 0)), 1)
    per_group = weight_two.shape[3]
    group_count = width_out // per_group
    second = lax.conv_general_dilated(
        padded[None],
        weight_two,
        (1, 1, 1),
        ((0, 0), (0, 0), (1, 1)),
        dimension_numbers=("NDHWC", "DHWIO", "NDHWC"),
        feature_group_count=group_count,
        preferred_element_type=jnp.float32,
    )[0]
    grouped = (second + bias_two).astype(jnp.bfloat16)
    return (activated, grouped)


def solution(mesh):
    in_specs = (P("chan", "slab", None, None), P(None, None, None, "chan", None), P(), P(), P())
    out_specs = (P("slab", "chan", None, None), P("slab", "chan", None, None))
    return jax.shard_map(local, mesh=mesh, in_specs=in_specs, out_specs=out_specs, check_vma=False)
```

profile of v0, /device:TPU:1, one launch (start us, length us, event | category | flops | bytes accessed | tf_op | source)
XLA Modules:
  0.0 262.4 jit_solution(4839935474151382590)
XLA Ops:
  7.2 3.5 %copy.44 = bf16[32,2,128,128]{2,0,3,1:T(8,128)(2,1)S(1)} copy(bf16[32,2,128,128]{3,2,1,0:T(8,128)(2,1)} %param.5) | data formatting | bytes 4194304 | tf_op args[0]
  10.8 4.6 %collective-permute-start = (bf16[32,1,128,128]{2,0,3,1:T(8,128)(2,1)S(1)}, bf16[32,1,128,128]{2,0,3,1:T(8,128)(2,1)S(1)}, u32[]{:S(2)}, u32[]{:S(2)}) collective-permute-start(bf16[32,1,128,128]{2,0,3,1:T(8,128)(2,1)S(1)} %slice.14), channel_id=1, source_target_pairs={{0,1},{1,2},{2,3},{3,4},{4,5},{5,6},{6,7},{8,9},{9,10},{10,11},{11... | collective-permute-start | bytes 3145736 | tf_op jit(solution)/shard_map/ppermute | solution.py:10
  15.4 11.7 %collective-permute-done = bf16[32,1,128,128]{2,0,3,1:T(8,128)(2,1)S(1)} collective-permute-done((bf16[32,1,128,128]{2,0,3,1:T(8,128)(2,1)S(1)}, bf16[32,1,128,128]{2,0,3,1:T(8,128)(2,1)S(1)}, u32[]{:S(2)}, u32[]{:S(2)}) %collective-permute-start) | collective-permute-done | bytes 1048608 | tf_op jit(solution)/shard_map/ppermute | solution.py:10
  27.4 2.3 pad
  29.8 21.8 %copy.47 = bf16[32,3,128,1,8,18]{0,4,5,2,1,3:T(8,128)(2,1)} copy(bf16[32,3,128,1,8,18]{2,0,5,4,1,3:T(8,128)(2,1)} %bitcast.30) | data formatting | bytes 7077888 | tf_op jit(solution)/shard_map/conv_general_dilated | solution.py:35
  51.6 1.9 slice.15
  53.5 12.0 %select_convert_fusion = bf16[1,64,8,9,256]{4,2,3,1,0:T(8,128)(2,1)S(1)} fusion(pred[8,9]{0,1:T(8,128)(4,1)S(1)} %copy-done.9, bf16[3,3,3,32,256]{4,3,2,1,0:T(8,128)(2,1)S(1)} %copy-done, bf16[32,3,128,1,7,2]{0,4,5,2,1,3:T(8,128)(2,1)S(1)} %slice.15, bf16[32,3,128,1,8,18]{0,4,5,2,1,3:T(8,128)(2,1)} %copy.47), kind=kOutput, calls=%fused_computation.10 | convolution fusion | flops 2041970688 | bytes 6684744 | tf_op jit(solution)/shard_map/conv_general_dilated | solution.py:35
  66.3 6.7 %copy.56 = bf16[1,64,64,256]{1,2,0,3:T(8,128)(2,1)} copy(bf16[1,64,64,256]{3,1,2,0:T(8,128)(2,1)S(1)} %slice_bitcast_fusion) | data formatting | bytes 4194304
  73.0 6.6 %reshape.58 = bf16[256,4096]{1,0:T(8,128)(2,1)} reshape(bf16[256,1,64,64]{3,2,1,0:T(8,128)(2,1)} %bitcast.29) | data formatting | bytes 4194304
  79.7 37.1 %reduce-scatter.4.cloned.1.call-done = bf16[64,4096]{1,0:T(8,128)(2,1)} async-done(((bf16[256,4096]{1,0:T(8,128)(2,1)}), bf16[64,4096]{1,0:T(8,128)(2,1)}) %reduce-scatter.4.cloned.1.call-update) | async-done | bytes 524304
  116.9 2.1 reshape.59
  118.9 1.2 copy.57
  120.6 0.7 copy.61
  121.3 1.0 reshape.60
  122.3 9.6 %all_to_all.18 = bf16[4,2,32768]{2,1,0:T(2,128)(2,1)S(1)} all-to-all(bf16[4,2,32768]{2,1,0:T(2,128)(2,1)S(1)} %reshape.60), channel_id=1, replica_groups=mesh['chan'=4,'slab'=8] {'chan'}, dimensions={0} | all-to-all | bytes 1048576 | tf_op jit(solution)/shard_map/all_to_all | solution.py:60
  131.9 0.7 reshape.61
  132.7 0.9 copy.50
  134.3 2.9 %collective-permute-start.1 = (bf16[1,1,64,256]{3,2,1,0:T(8,128)(2,1)S(1)}, bf16[1,1,64,256]{3,2,1,0:T(8,128)(2,1)S(1)}, u32[]{:S(2)}, u32[]{:S(2)}) collective-permute-start(bf16[1,1,64,256]{3,2,1,0:T(8,128)(2,1)S(1)} %get-tuple-element.11), channel_id=1, source_target_pairs={{0,8},{8,16},{16,24},{1,9},{9,17},{17,25},{2,10},{10,18},{18,26},{... | collective-permute-start | bytes 98312 | tf_op jit(solution)/shard_map/ppermute | solution.py:21
  137.2 1.3 collective-permute-start.2
  138.5 3.5 %collective-permute-done.2 = bf16[1,1,64,256]{3,2,1,0:T(8,128)(2,1)S(1)} collective-permute-done((bf16[1,1,64,256]{3,2,1,0:T(8,128)(2,1)S(1)}, bf16[1,1,64,256]{3,2,1,0:T(8,128)(2,1)S(1)}, u32[]{:S(2)}, u32[]{:S(2)}) %collective-permute-start.2) | collective-permute-done | bytes 32800 | tf_op jit(solution)/shard_map/ppermute | solution.py:23
  142.0 5.0 %collective-permute-start.4 = (bf16[1,18,64,256]{3,2,1,0:T(8,128)(2,1)S(1)}, bf16[1,18,64,256]{3,2,1,0:T(8,128)(2,1)S(1)}, u32[]{:S(2)}, u32[]{:S(2)}) collective-permute-start(bf16[1,18,64,256]{3,2,1,0:T(8,128)(2,1)S(1)} %constant_dynamic-update-slice_fusion), channel_id=1, source_target_pairs={{1,0},{2,1},{3,2},{4,3},{5,4},{6,5},{7,6},{9,8},{10,9},{11,10},{12... | collective-permute-start | bytes 1769480 | tf_op jit(solution)/shard_map/ppermute | solution.py:23
  147.1 3.0 %collective-permute-start.3 = (bf16[1,18,64,256]{3,2,1,0:T(8,128)(2,1)S(1)}, bf16[1,18,64,256]{3,2,1,0:T(8,128)(2,1)}, u32[]{:S(2)}, u32[]{:S(2)}) collective-permute-start(bf16[1,18,64,256]{3,2,1,0:T(8,128)(2,1)S(1)} %constant_dynamic-update-slice_fusion), channel_id=1, source_target_pairs={{0,1},{1,2},{2,3},{3,4},{4,5},{5,6},{6,7},{8,9},{9,10},{10,11},{11... | collective-permute-start | bytes 1769480 | tf_op jit(solution)/shard_map/ppermute | solution.py:21
  150.1 1.7 shard_map.70
  151.8 3.9 %collective-permute-done.4 = bf16[1,18,64,256]{3,2,1,0:T(8,128)(2,1)S(1)} collective-permute-done((bf16[1,18,64,256]{3,2,1,0:T(8,128)(2,1)S(1)}, bf16[1,18,64,256]{3,2,1,0:T(8,128)(2,1)S(1)}, u32[]{:S(2)}, u32[]{:S(2)}) %collective-permute-start.4) | collective-permute-done | bytes 589856 | tf_op jit(solution)/shard_map/ppermute | solution.py:23
  155.7 0.8 copy-done.5
  156.9 1.6 pad_maximum_fusion
  158.5 3.1 %copy.51 = bf16[3,18,64,256]{2,3,1,0:T(8,128)(2,1)} copy(bf16[3,18,64,256]{3,2,1,0:T(8,128)(2,1)S(1)} %pad_maximum_fusion) | data formatting | bytes 3538944 | tf_op jit(solution)/shard_map/concatenate | solution.py:19
  161.7 30.9 %copy.52 = bf16[1,3,18,64,8,32]{5,0,4,3,2,1:T(2,128)(2,1)} copy(bf16[1,3,18,64,8,32]{3,5,4,2,1,0:T(8,128)(2,1)} %bitcast.31) | data formatting | bytes 3538944 | tf_op jit(solution)/shard_map/broadcast_in_dim | solution.py:65
  192.6 50.4 %fusion.12 = f32[1,1,16,64,8,32]{5,0,4,3,2,1:T(1,128)} fusion(bf16[1,3,18,64,8,32]{5,0,4,3,2,1:T(2,128)(2,1)} %copy.52, bf16[3,3,3,32,8,32]{5,4,3,2,1,0:T(8,128)(2,1)S(1)} %copy-done.3), kind=kOutput, calls=%fused_computation.16 | convolution fusion | flops 448266240 | bytes 3260416 | tf_op jit(solution)/shard_map/conv_general_dilated | solution.py:64
  243.0 8.9 %copy.54 = f32[1,1,16,64,8,32]{3,5,4,2,1,0:T(8,128)S(1)} copy(f32[1,1,16,64,8,32]{5,0,4,3,2,1:T(1,128)} %fusion.12) | data formatting | bytes 2097152 | tf_op jit(solution)/shard_map/conv_general_dilated | solution.py:64
  251.9 1.3 add_convert_fusion
  253.2 2.3 copy.55
  (34 shorter events, 2.8 us)
Async XLA Ops:
  7.2 46.3 %copy-start = (bf16[3,3,3,32,256]{4,3,2,1,0:T(8,128)(2,1)S(1)}, bf16[3,3,3,32,256]{4,3,2,1,0:T(8,128)(2,1)}, u32[]{:S(2)}) copy-start(bf16[3,3,3,32,256]{4,3,2,1,0:T(8,128)(2,1)} %param.6) | copy-start | bytes 1327108
  7.2 109.7 %reduce-scatter.4.cloned.1.call-start = ((), (), s32[]{:S(2)}) async-start(), calls=%async_computation.2 | async-start | bytes 2621440
  10.8 16.3 %collective-permute-start = (bf16[32,1,128,128]{2,0,3,1:T(8,128)(2,1)S(1)}, bf16[32,1,128,128]{2,0,3,1:T(8,128)(2,1)S(1)}, u32[]{:S(2)}, u32[]{:S(2)}) collective-permute-start(bf16[32,1,128,128]{2,0,3,1:T(8,128)(2,1)S(1)} %slice.14), channel_id=1, source_target_pairs={{0,1},{1,2},{2,3},{3,4},{4,5},{5,6},{6,7},{8,9},{9,10},{10,11},{11... | collective-permute-start | bytes 3145736 | tf_op jit(solution)/shard_map/ppermute | solution.py:10
  51.6 1.9 copy-start.9
  73.0 6.7 %copy-start.8 = (f32[256]{0:T(256)S(1)}, f32[256]{0:T(256)}, u32[]{:S(2)}) copy-start(f32[256]{0:T(256)} %param.7) | copy-start | bytes 3076
  132.7 17.4 %copy-start.6 = (bf16[3,3,3,32,256]{4,3,2,1,0:T(8,128)(2,1)S(1)}, bf16[3,3,3,32,256]{4,3,2,1,0:T(8,128)(2,1)}, u32[]{:S(2)}) copy-start(bf16[3,3,3,32,256]{4,3,2,1,0:T(8,128)(2,1)} %param.8) | copy-start | bytes 1327108
  134.2 24.3 %copy-start.2 = (bf16[1,16,64,256]{3,2,1,0:T(8,128)(2,1)}, bf16[1,16,64,256]{3,2,1,0:T(8,128)(2,1)S(1)}, u32[]{:S(2)}) copy-start(bf16[1,16,64,256]{3,2,1,0:T(8,128)(2,1)S(1)} %all_to_all.16) | copy-start | bytes 1572868
  134.3 4.2 %collective-permute-start.1 = (bf16[1,1,64,256]{3,2,1,0:T(8,128)(2,1)S(1)}, bf16[1,1,64,256]{3,2,1,0:T(8,128)(2,1)S(1)}, u32[]{:S(2)}, u32[]{:S(2)}) collective-permute-start(bf16[1,1,64,256]{3,2,1,0:T(8,128)(2,1)S(1)} %get-tuple-element.11), channel_id=1, source_target_pairs={{0,8},{8,16},{16,24},{1,9},{9,17},{17,25},{2,10},{10,18},{18,26},{... | collective-permute-start | bytes 98312 | tf_op jit(solution)/shard_map/ppermute | solution.py:21
  137.2 4.9 %collective-permute-start.2 = (bf16[1,1,64,256]{3,2,1,0:T(8,128)(2,1)S(1)}, bf16[1,1,64,256]{3,2,1,0:T(8,128)(2,1)S(1)}, u32[]{:S(2)}, u32[]{:S(2)}) collective-permute-start(bf16[1,1,64,256]{3,2,1,0:T(8,128)(2,1)S(1)} %get-tuple-element.10), channel_id=1, source_target_pairs={{8,0},{16,8},{24,16},{9,1},{17,9},{25,17},{10,2},{18,10},{26,18},{... | collective-permute-start | bytes 98312 | tf_op jit(solution)/shard_map/ppermute | solution.py:23
  142.0 13.7 %copy-start.4 = (bf16[1,18,64,256]{3,2,1,0:T(8,128)(2,1)}, bf16[1,18,64,256]{3,2,1,0:T(8,128)(2,1)S(1)}, u32[]{:S(2)}) copy-start(bf16[1,18,64,256]{3,2,1,0:T(8,128)(2,1)S(1)} %constant_dynamic-update-slice_fusion) | copy-start | bytes 1769476
  142.0 13.7 %collective-permute-start.4 = (bf16[1,18,64,256]{3,2,1,0:T(8,128)(2,1)S(1)}, bf16[1,18,64,256]{3,2,1,0:T(8,128)(2,1)S(1)}, u32[]{:S(2)}, u32[]{:S(2)}) collective-permute-start(bf16[1,18,64,256]{3,2,1,0:T(8,128)(2,1)S(1)} %constant_dynamic-update-slice_fusion), channel_id=1, source_target_pairs={{1,0},{2,1},{3,2},{4,3},{5,4},{6,5},{7,6},{9,8},{10,9},{11,10},{12... | collective-permute-start | bytes 1769480 | tf_op jit(solution)/shard_map/ppermute | solution.py:23
  147.1 9.8 %collective-permute-start.3 = (bf16[1,18,64,256]{3,2,1,0:T(8,128)(2,1)S(1)}, bf16[1,18,64,256]{3,2,1,0:T(8,128)(2,1)}, u32[]{:S(2)}, u32[]{:S(2)}) collective-permute-start(bf16[1,18,64,256]{3,2,1,0:T(8,128)(2,1)S(1)} %constant_dynamic-update-slice_fusion), channel_id=1, source_target_pairs={{0,1},{1,2},{2,3},{3,4},{4,5},{5,6},{6,7},{8,9},{9,10},{10,11},{11... | collective-permute-start | bytes 1769480 | tf_op jit(solution)/shard_map/ppermute | solution.py:21
  155.7 0.8 copy-start.5
  161.7 30.9 %copy-start.3 = (bf16[3,3,3,32,8,32]{5,4,3,2,1,0:T(8,128)(2,1)S(1)}, bf16[3,3,3,32,8,32]{5,4,3,2,1,0:T(8,128)(2,1)}, u32[]{:S(2)}) copy-start(bf16[3,3,3,32,8,32]{5,4,3,2,1,0:T(8,128)(2,1)} %shard_map.70) | copy-start | bytes 1327108
  243.0 8.9 %copy-start.7 = (f32[256]{0:T(256)S(1)}, f32[256]{0:T(256)}, u32[]{:S(2)}) copy-start(f32[256]{0:T(256)} %param.9) | copy-start | bytes 3076
  251.9 3.7 %copy-start.1 = (bf16[3,3,3,32,256]{4,3,2,1,0:T(8,128)(2,1)S(1)}, bf16[3,3,3,32,256]{4,3,2,1,0:T(8,128)(2,1)}, u32[]{:S(2)}) copy-start(bf16[3,3,3,32,256]{4,3,2,1,0:T(8,128)(2,1)} %param.6) | copy-start | bytes 1327108
Sparse Core Ops, SparseCore 0:
  79.7 37.0 reduce-scatter.3
where the time goes:
time: 266 us; the launch traced here: 262 us
  local copies, waits for them, and re-layouts  98.9 us (37%)
  matrix products  62.4 us (23%)
  waiting for transfers between devices  56.6 us (21%)
  starting transfers between devices  16.9 us (6%)
  between operations  14.3 us (5%)
  blocking collectives  9.63 us (4%)
  other arithmetic  3.58 us (1%)
    conv_general_dilated x1, matrix products, local(): lax.conv_general_dilated(padded[None], weight_two, (1, 1, 1), ((0, 0), (0...  50.4 us
    unnamed x2, waiting for transfers between devices  37.2 us
    broadcast_in_dim x1, local copies, waits for them, and re-layouts, local(): padded[None]  30.9 us
    unnamed x30, local copies, waits for them, and re-layouts  25.1 us
    conv_general_dilated x2, local copies, waits for them, and re-layouts, strided_conv(): lax.conv_general_dilated(source[None], kernel, (2, 2, 2), padding, dimens...  23.7 us
    conv_general_dilated x1, matrix products, strided_conv(): lax.conv_general_dilated(source[None], kernel, (2, 2, 2), padding, dimens...  12 us
    ppermute x1, waiting for transfers between devices, shifted(): return lax.ppermute(block, axis, route)  11.7 us
    all_to_all x1, blocking collectives, local(): lax.all_to_all(act_part, 'chan', split_axis=1, concat_axis=3, tiled=True)  9.63 us
  transfers between devices with their start and end apart: 6, of which 5 were waited for; matrix products, arithmetic and copies ran while one was open for 1% of the time, Pallas kernels for 0%

commit v1 on v0

v1 whole, which is shorter than its diff:
```python
import functools

import jax
import jax.numpy as jnp
from jax import lax
from jax.experimental import pallas as pl
from jax.experimental.pallas import tpu as pltpu
from jax.sharding import PartitionSpec as P

BF = jnp.bfloat16
F32 = jnp.float32
MESH = pl.DeviceIdType.MESH
AROUND = [(0, 1), (0, -1), (1, 0), (-1, 0), (1, 1), (1, -1), (-1, 1), (-1, -1)]


def leaky(value):
    return jnp.where(value > 0, value, 0.3 * value)


def body(parts, slabs, own_ref, k1_ref, b1_ref, k2_ref, b2_ref, act_ref, out_ref,
         low_ref, t_ref, part_ref, recv_ref, a_ref, w1_ref, w2_ref, acc_ref,
         low_send, low_recv, sum_send, sum_recv, halo_send, halo_recv):
    c = own_ref.shape[2]
    tall = 128 // c
    wins = own_ref.shape[1] // tall
    half = own_ref.shape[3] // 2
    mine, q, k = act_ref.shape
    outs = tall // 2
    step = 4 * outs if mine % (4 * outs) == 0 else mine
    pieces = mine // step
    me, slab = lax.axis_index("chan"), lax.axis_index("slab")

    def peer(s):
        if parts == 4:
            return 2 * lax.rem(me // 2 + lax.div(s, 2), 2) + lax.rem(lax.rem(me, 2) + lax.rem(s, 2), 2)
        return lax.rem(me + s, parts)

    def inside(dc, ds):
        ok = None
        for coord, move, size in ((me, dc, parts), (slab, ds, slabs)):
            if move:
                one = coord + move < size if move > 0 else coord + move >= 0
                ok = one if ok is None else jnp.logical_and(ok, one)
        return ok

    barrier = pltpu.get_barrier_semaphore()
    for s in range(1, parts):
        pl.semaphore_signal(barrier, inc=1, device_id={"chan": peer(jnp.int32(s)), "slab": slab}, device_id_type=MESH)
    for dc, ds in AROUND:
        if ds:
            @pl.when(inside(dc, ds))
            def _(dc=dc, ds=ds):
                pl.semaphore_signal(barrier, inc=1, device_id={"chan": me + dc, "slab": slab + ds}, device_id_type=MESH)
    one = jnp.int32(1)
    across = jnp.minimum(slab, one) + jnp.minimum(jnp.int32(slabs - 1) - slab, one)
    along = one + jnp.minimum(me, one) + jnp.minimum(jnp.int32(parts - 1) - me, one)
    pl.semaphore_wait(barrier, jnp.int32(parts - 1) + across * along)

    def low_copy():
        return pltpu.make_async_remote_copy(
            src_ref=own_ref.at[own_ref.shape[0] - 1], dst_ref=low_ref, send_sem=low_send, recv_sem=low_recv,
            device_id={"chan": me, "slab": slab + 1}, device_id_type=MESH)

    @pl.when(slab + 1 < slabs)
    def _():
        low_copy().start()

    w1_ref[...] = jnp.zeros_like(w1_ref)
    for e in range(9):
        i, l = divmod(e, 3)
        for par in range(outs):
            for j in range(3):
                start = e * 256 + (tall - 1 + 2 * par + j) * c
                w1_ref[start:start + c, par * k:(par + 1) * k] = k1_ref[i, j, l]
    m = k2_ref.shape[3]
    group = lax.broadcasted_iota(jnp.int32, (m, k), 1) // m
    for i in range(3):
        for l in range(3):
            for j in range(3):
                taps = k2_ref[i, j, l]
                for g in range(k // m):
                    w2_ref[i, l, j * k + g * m:j * k + (g + 1) * m] = jnp.where(group == g, taps, jnp.zeros_like(taps))
    width = own_ref.shape[3]
    spot = lax.broadcasted_iota(jnp.int32, (half, width), 1) - 2 * lax.broadcasted_iota(jnp.int32, (half, width), 0)
    sel = jnp.concatenate([jnp.where(spot == l - 1, 1.0, 0.0) for l in range(3)], axis=0).astype(BF)
    for e in range(9):
        t_ref[e, 0] = jnp.zeros_like(t_ref[e, 0])

    def decimate(d):
        def go(b, carry):
            rows = pl.ds(4 * tall * b, 4 * tall)
            x = low_ref[rows] if d == 0 else own_ref[d - 1, rows]
            x = x.reshape(512, own_ref.shape[3])
            t = lax.dot_general(sel, x, (((1,), (1,)), ((), ())), preferred_element_type=F32).astype(BF)
            for l in range(3):
                for u in range(4):
                    t_ref[3 * d + l, 4 * b + u + 1] = t[l * half:(l + 1) * half, 128 * u:128 * (u + 1)]
            return carry

        lax.fori_loop(0, wins // 4, go, 0)

    decimate(1)
    decimate(2)

    @pl.when(slab == 0)
    def _():
        low_ref[...] = jnp.zeros_like(low_ref)

    @pl.when(slab > 0)
    def _():
        low_copy().wait_recv()

    decimate(0)

    def chunk(b):
        lhs = []
        for e in range(9):
            lhs.append(t_ref[e, pl.ds(4 * b, 4)].reshape(4 * half, 128))
            lhs.append(t_ref[e, pl.ds(4 * b + 1, 4)].reshape(4 * half, 128))
        res = jnp.dot(jnp.concatenate(lhs, axis=1), w1_ref[...], preferred_element_type=F32).astype(BF)
        for u in range(4):
            for par in range(outs):
                part_ref[4 * outs * b + outs * u + par] = res[u * half:(u + 1) * half, par * k:(par + 1) * k]

    def sum_copy(s, h):
        to = peer(s)
        return pltpu.make_async_remote_copy(
            src_ref=part_ref.at[pl.ds(to * mine + h * step, step)], dst_ref=recv_ref.at[s - 1, pl.ds(h * step, step)],
            send_sem=sum_send.at[s - 1, h], recv_sem=sum_recv.at[s - 1, h],
            device_id={"chan": to, "slab": slab}, device_id_type=MESH)

    if step == 4 * outs:
        def one(n, carry):
            s, h = parts - 1 - lax.div(n, pieces), lax.rem(n, pieces)
            chunk(peer(s) * pieces + h)

            @pl.when(n < (parts - 1) * pieces)
            def _():
                sum_copy(s, h).start()
            return carry

        lax.fori_loop(0, parts * pieces, one, 0)
    else:
        def one(n, carry):
            chunk(n)
            return carry

        lax.fori_loop(0, wins // 4, one, 0)
        for s in range(1, parts):
            sum_copy(jnp.int32(s), 0).start()

    for h in range(pieces):
        for s in range(1, parts):
            sum_copy(jnp.int32(s), h).wait_recv()
        for r in range(h * step, (h + 1) * step, 4):
            total = part_ref[pl.ds(me * mine + r, 4)].astype(F32)
            for s in range(1, parts):
                total += recv_ref[s - 1, r:r + 4].astype(F32)
            act = leaky(total + b1_ref[...]).astype(BF)
            act_ref[r:r + 4] = act
            a_ref[1, r + 1:r + 5] = act

    def spots(dc, ds):
        if dc == 0:
            return a_ref.at[1, pl.ds(1, mine)], a_ref.at[1 - ds, pl.ds(1, mine)]
        return a_ref.at[1, pl.ds(mine if dc > 0 else 1, 1)], a_ref.at[1 - ds, pl.ds(0 if dc > 0 else mine + 1, 1)]

    def halo_copy(n):
        dc, ds = AROUND[n]
        src, dst = spots(dc, ds)
        return pltpu.make_async_remote_copy(
            src_ref=src, dst_ref=dst, send_sem=halo_send.at[n], recv_sem=halo_recv.at[n],
            device_id={"chan": me + dc, "slab": slab + ds}, device_id_type=MESH)

    def arrive(n):
        dc, ds = AROUND[n]
        there = inside(-dc, -ds)

        @pl.when(there)
        def _():
            halo_copy(n).wait_recv()

        @pl.when(jnp.logical_not(there))
        def _():
            dst = spots(dc, ds)[1]
            dst[...] = jnp.zeros(dst.shape, BF)

    for n, (dc, ds) in enumerate(AROUND):
        @pl.when(inside(dc, ds))
        def _(n=n):
            halo_copy(n).start()

    for i, last in ((1, False), (0, False), (2, True)):
        for n, (dc, ds) in enumerate(AROUND):
            if 1 - ds == i:
                arrive(n)

        def rows4(b, carry, i=i, last=last):
            lhs = jnp.concatenate([a_ref[i, pl.ds(4 * b + j, 4)].reshape(4 * q, k) for j in range(3)], axis=1)
            here = pl.ds(4 * q * b, 4 * q)
            accs = []
            for l in range(3):
                acc = jnp.dot(lhs, w2_ref[i, l], preferred_element_type=F32)
                if i != 1:
                    acc += acc_ref[l, here]
                accs.append(acc)
            if not last:
                for l in range(3):
                    acc_ref[l, here] = accs[l]
                return carry
            col = lax.rem(lax.broadcasted_iota(jnp.int32, (4 * q, k), 0), q)
            left = jnp.where(col == 0, 0.0, pltpu.roll(accs[0], 1, 0))
            right = jnp.where(col == q - 1, 0.0, pltpu.roll(accs[2], 4 * q - 1, 0))
            res = left + accs[1] + right + b2_ref[...]
            out_ref[pl.ds(4 * b, 4)] = res.reshape(4, q, k).astype(BF)
            return carry

        lax.fori_loop(0, mine // 4, rows4, 0)

    @pl.when(slab + 1 < slabs)
    def _():
        low_copy().wait_send()
    for s in range(1, parts):
        for h in range(pieces):
            sum_copy(jnp.int32(s), h).wait_send()
    for n, (dc, ds) in enumerate(AROUND):
        @pl.when(inside(dc, ds))
        def _(n=n):
            halo_copy(n).wait_send()


def local(volume, weight_one, bias_one, weight_two, bias_two):
    c, planes, height, width = volume.shape
    k = weight_one.shape[4]
    parts, slabs = lax.axis_size("chan"), lax.axis_size("slab")
    own_t = volume.transpose(1, 2, 0, 3)
    rows, cols = height // 2, width // 2
    mine = rows // parts
    step = 256 // c if mine % (256 // c) == 0 else mine
    vmem = pl.BlockSpec(memory_space=pltpu.VMEM)
    dma = pltpu.SemaphoreType.DMA
    block = jax.ShapeDtypeStruct((mine, cols, k), BF)
    act, grouped = pl.pallas_call(
        functools.partial(body, parts, slabs),
        out_shape=(block, block),
        in_specs=[vmem] * 5,
        out_specs=(vmem, vmem),
        scratch_shapes=[
            pltpu.VMEM((height, c, width), BF),
            pltpu.VMEM((9, height * c // 128 + 1, cols, 128), BF),
            pltpu.VMEM((rows, cols, k), BF),
            pltpu.VMEM((parts - 1, mine, cols, k), BF),
            pltpu.VMEM((3, mine + 2, cols, k), BF),
            pltpu.VMEM((9 * 256, 64 // c * k), BF),
            pltpu.VMEM((3, 3, 3 * k, k), BF),
            pltpu.VMEM((3, mine * cols, k), F32),
            dma, dma,
            dma((parts - 1, mine // step)), dma((parts - 1, mine // step)),
            dma((8,)), dma((8,)),
        ],
        compiler_params=pltpu.CompilerParams(vmem_limit_bytes=48 << 20, collective_id=0, has_side_effects=True),
    )(own_t, weight_one, bias_one.reshape(1, k), weight_two, bias_two.reshape(1, k))
    return act[None], grouped[None]


def solution(mesh):
    in_specs = (P("chan", "slab", None, None), P(None, None, None, "chan", None), P(), P(), P())
    out_specs = (P("slab", "chan", None, None), P("slab", "chan", None, None))
    return jax.shard_map(local, mesh=mesh, in_specs=in_specs, out_specs=out_specs, check_vma=False)
```

time: 266 us -> 53.3 us (0.20); the launches traced: 262 us -> 53.2 us
  local copies, waits for them, and re-layouts: 98.9 us -> 4.62 us
  matrix products: 62.4 us -> 0 us
  waiting for transfers between devices: 56.6 us -> 0 us
  Pallas kernels: 0 us -> 47.8 us
  starting transfers between devices: 16.9 us -> 0 us
  between operations: 14.3 us -> 0.7 us
  blocking collectives: 9.63 us -> 0 us
  other arithmetic: 3.58 us -> 0 us
    conv_general_dilated x2 -> x0, matrix products: 62.4 us -> none  [the longest x1 50.4 us: local(): lax.conv_general_dilated(padded[None], weight_two, (1, 1, 1), ((0, 0), (0...]
    pallas_call x0 -> x1, Pallas kernels: none -> 47.8 us  [local(): pl.pallas_call(functools.partial(body, parts, slabs), out_shape=(block, b...]
    unnamed x2 -> x0, waiting for transfers between devices: 37.2 us -> none
    broadcast_in_dim x2 -> x0, local copies, waits for them, and re-layouts: 33.3 us -> none  [the longest x1 30.9 us: local(): padded[None]]
    conv_general_dilated x3 -> x0, local copies, waits for them, and re-layouts: 32.5 us -> none  [the longest x2 23.7 us: strided_conv(): lax.conv_general_dilated(source[None], kernel, (2, 2, 2), padding, dimens...]
    unnamed x30 -> x11, local copies, waits for them, and re-layouts: 25.1 us -> 4.62 us
    ppermute x5 -> x0, waiting for transfers between devices: 19.5 us -> none  [the longest x1 11.7 us: shifted(): return lax.ppermute(block, axis, route)]
    ppermute x5 -> x0, starting transfers between devices: 16.8 us -> none  [the longest x2 6.32 us: with_halo(): lax.ppermute(head, axis, [((i + 1) % count, i) for i in range(ends)])]
  transfers between devices with their start and end apart: 6 -> 0, of which waited for: 5 -> 0; matrix products, arithmetic and copies ran while one was open for 1% -> 0% of each run, Pallas kernels for 0% -> 0%
where the time goes in v1:
time: 53.3 us; the launch traced here: 53.2 us
  Pallas kernels  47.8 us (90%)
  local copies, waits for them, and re-layouts  4.62 us (9%)
  between operations  0.7 us (1%)
    pallas_call x1, Pallas kernels, local(): pl.pallas_call(functools.partial(body, parts, slabs), out_shape=(block, b...  47.8 us
    unnamed x11, local copies, waits for them, and re-layouts  4.62 us

profile of v1, /device:TPU:1, one launch (start us, length us, event | category | flops | bytes accessed | tf_op | source)
XLA Modules:
  0.0 53.2 jit_solution(16319185413530543913)
XLA Ops:
  0.6 0.0 copy-start
  0.6 0.0 copy-start.1
  0.7 0.0 copy-start.2
  0.7 0.0 copy-start.3
  0.7 3.0 %copy.9 = bf16[32,2,128,128]{3,0,2,1:T(8,128)(2,1)S(1)} copy(bf16[32,2,128,128]{3,2,1,0:T(8,128)(2,1)} %param.5) | data formatting | bytes 4194304 | tf_op args[0]
  3.7 0.0 copy-done
  3.7 0.0 copy-done.1
  3.7 0.0 copy-done.2
  3.7 0.0 copy-done.3
  3.7 47.8 %shard_map.68 = (bf16[16,64,256]{2,1,0:T(8,128)(2,1)S(1)}, bf16[16,64,256]{2,1,0:T(8,128)(2,1)S(1)}) custom-call(bf16[2,128,32,128]{3,2,1,0:T(8,128)(2,1)S(1)} %bitcast.7, bf16[3,3,3,32,256]{4,3,2,1,0:T(8,128)(2,1)S(1)} %copy-done, f32[1,256]{1,0:T(1,128)S(1)} %bitcast.10, bf16[3,3,3,32,256]{4,3,2,1,0:T(8,128)(2,1)S(1)} %copy-done.1, f32[1,256]{1,0:T(1,128)S(1)} %bitcast.11), custom_call_target="tpu_custom_call" | custom-call | tf_op jit(solution)/shard_map/pallas_call | solution.py:243
  51.6 0.8 %copy.12 = bf16[1,16,64,256]{3,2,1,0:T(8,128)(2,1)} copy(bf16[1,16,64,256]{3,2,1,0:T(8,128)(2,1)S(1)} %bitcast.9) | data formatting | bytes 1048576
  52.4 0.8 %copy.13 = bf16[1,16,64,256]{3,2,1,0:T(8,128)(2,1)} copy(bf16[1,16,64,256]{3,2,1,0:T(8,128)(2,1)S(1)} %bitcast.8) | data formatting | bytes 1048576
Async XLA Ops:
  0.6 3.1 %copy-start = (bf16[3,3,3,32,256]{4,3,2,1,0:T(8,128)(2,1)S(1)}, bf16[3,3,3,32,256]{4,3,2,1,0:T(8,128)(2,1)}, u32[]{:S(2)}) copy-start(bf16[3,3,3,32,256]{4,3,2,1,0:T(8,128)(2,1)} %k1_ref.1) | copy-start | bytes 1327108
  0.6 3.1 %copy-start.1 = (bf16[3,3,3,32,256]{4,3,2,1,0:T(8,128)(2,1)S(1)}, bf16[3,3,3,32,256]{4,3,2,1,0:T(8,128)(2,1)}, u32[]{:S(2)}) copy-start(bf16[3,3,3,32,256]{4,3,2,1,0:T(8,128)(2,1)} %k2_ref.1) | copy-start | bytes 1327108
  0.7 3.1 %copy-start.2 = (f32[256]{0:T(256)S(1)}, f32[256]{0:T(256)}, u32[]{:S(2)}) copy-start(f32[256]{0:T(256)} %param.7) | copy-start | bytes 3076
  0.7 3.1 %copy-start.3 = (f32[256]{0:T(256)S(1)}, f32[256]{0:T(256)}, u32[]{:S(2)}) copy-start(f32[256]{0:T(256)} %param.9) | copy-start | bytes 3076

commit v2 on v1

--- a/solution.py
+++ b/solution.py
@@ -130,16 +130,18 @@
             device_id={"chan": to, "slab": slab}, device_id_type=MESH)
 
     if step == 4 * outs:
-        def one(n, carry):
-            s, h = parts - 1 - lax.div(n, pieces), lax.rem(n, pieces)
+        def away(n, carry):
+            s, h = parts - 1 - lax.rem(n, parts - 1), lax.div(n, parts - 1)
             chunk(peer(s) * pieces + h)
-
-            @pl.when(n < (parts - 1) * pieces)
-            def _():
-                sum_copy(s, h).start()
-            return carry
-
-        lax.fori_loop(0, parts * pieces, one, 0)
+            sum_copy(s, h).start()
+            return carry
+
+        def home(h, carry):
+            chunk(me * pieces + h)
+            return carry
+
+        lax.fori_loop(0, (parts - 1) * pieces, away, 0)
+        lax.fori_loop(0, pieces, home, 0)
     else:
         def one(n, carry):
             chunk(n)
@@ -148,6 +150,35 @@
         lax.fori_loop(0, wins // 4, one, 0)
         for s in range(1, parts):
             sum_copy(jnp.int32(s), 0).start()
+
+    def spots(dc, ds, h):
+        if dc == 0:
+            rows = pl.ds(1 + h * step, step)
+            return a_ref.at[1, rows], a_ref.at[1 - ds, rows]
+        return a_ref.at[1, pl.ds(mine if dc > 0 else 1, 1)], a_ref.at[1 - ds, pl.ds(0 if dc > 0 else mine + 1, 1)]
+
+    def halo_copy(n, h):
+        dc, ds = AROUND[n]
+        src, dst = spots(dc, ds, h)
+        return pltpu.make_async_remote_copy(
+            src_ref=src, dst_ref=dst, send_sem=halo_send.at[n, h], recv_sem=halo_recv.at[n, h],
+            device_id={"chan": me + dc, "slab": slab + ds}, device_id_type=MESH)
+
+    def due(dc):
+        return range(pieces) if dc == 0 else (pieces - 1,) if dc > 0 else (0,)
+
+    def arrive(n):
+        dc, ds = AROUND[n]
+        there = inside(-dc, -ds)
+        for h in due(dc):
+            @pl.when(there)
+            def _(h=h):
+                halo_copy(n, h).wait_recv()
+
+            @pl.when(jnp.logical_not(there))
+            def _(h=h):
+                dst = spots(dc, ds, h)[1]
+                dst[...] = jnp.zeros(dst.shape, BF)
 
     for h in range(pieces):
         for s in range(1, parts):
@@ -159,36 +190,11 @@
             act = leaky(total + b1_ref[...]).astype(BF)
             act_ref[r:r + 4] = act
             a_ref[1, r + 1:r + 5] = act
-
-    def spots(dc, ds):
-        if dc == 0:
-            return a_ref.at[1, pl.ds(1, mine)], a_ref.at[1 - ds, pl.ds(1, mine)]
-        return a_ref.at[1, pl.ds(mine if dc > 0 else 1, 1)], a_ref.at[1 - ds, pl.ds(0 if dc > 0 else mine + 1, 1)]
-
-    def halo_copy(n):
-        dc, ds = AROUND[n]
-        src, dst = spots(dc, ds)
-        return pltpu.make_async_remote_copy(
-            src_ref=src, dst_ref=dst, send_sem=halo_send.at[n], recv_sem=halo_recv.at[n],
-            device_id={"chan": me + dc, "slab": slab + ds}, device_id_type=MESH)
-
-    def arrive(n):
-        dc, ds = AROUND[n]
-        there = inside(-dc, -ds)
-
-        @pl.when(there)
-        def _():
-            halo_copy(n).wait_recv()
-
-        @pl.when(jnp.logical_not(there))
-        def _():
-            dst = spots(dc, ds)[1]
-            dst[...] = jnp.zeros(dst.shape, BF)
-
-    for n, (dc, ds) in enumerate(AROUND):
-        @pl.when(inside(dc, ds))
-        def _(n=n):
-            halo_copy(n).start()
+        for n, (dc, ds) in enumerate(AROUND):
+            if h in due(dc):
+                @pl.when(inside(dc, ds))
+                def _(n=n, h=h):
+                    halo_copy(n, h).start()
 
     for i, last in ((1, False), (0, False), (2, True)):
         for n, (dc, ds) in enumerate(AROUND):
@@ -224,9 +230,10 @@
         for h in range(pieces):
             sum_copy(jnp.int32(s), h).wait_send()
     for n, (dc, ds) in enumerate(AROUND):
-        @pl.when(inside(dc, ds))
-        def _(n=n):
-            halo_copy(n).wait_send()
+        for h in due(dc):
+            @pl.when(inside(dc, ds))
+            def _(n=n, h=h):
+                halo_copy(n, h).wait_send()
 
 
 def local(volume, weight_one, bias_one, weight_two, bias_two):
@@ -256,7 +263,7 @@
             pltpu.VMEM((3, mine * cols, k), F32),
             dma, dma,
             dma((parts - 1, mine // step)), dma((parts - 1, mine // step)),
-            dma((8,)), dma((8,)),
+            dma((8, mine // step)), dma((8, mine // step)),
         ],
         compiler_params=pltpu.CompilerParams(vmem_limit_bytes=48 << 20, collective_id=0, has_side_effects=True),
     )(own_t, weight_one, bias_one.reshape(1, k), weight_two, bias_two.reshape(1, k))

time: 53.3 us -> 50.8 us (0.953)
  Pallas kernels: 47.8 us -> 45.1 us
    pallas_call x1, Pallas kernels: 47.8 us -> 45.1 us  [local(): pl.pallas_call(functools.partial(body, parts, slabs), out_shape=(block, b...]
where the time goes in v2:
time: 50.8 us; the launch traced here: 50.4 us
  Pallas kernels  45.1 us (89%)
  local copies, waits for them, and re-layouts  4.62 us (9%)
  between operations  0.7 us (1%)
    pallas_call x1, Pallas kernels, local(): pl.pallas_call(functools.partial(body, parts, slabs), out_shape=(block, b...  45.1 us
    unnamed x11, local copies, waits for them, and re-layouts  4.62 us

profile of v2, /device:TPU:1, one launch (start us, length us, event | category | flops | bytes accessed | tf_op | source)
XLA Modules:
  0.0 50.4 jit_solution(16228612248960239882)
XLA Ops:
  0.6 0.0 copy-start
  0.6 0.0 copy-start.1
  0.7 0.0 copy-start.2
  0.7 0.0 copy-start.3
  0.7 3.0 %copy.9 = bf16[32,2,128,128]{3,0,2,1:T(8,128)(2,1)S(1)} copy(bf16[32,2,128,128]{3,2,1,0:T(8,128)(2,1)} %param.5) | data formatting | bytes 4194304 | tf_op args[0]
  3.7 0.0 copy-done
  3.7 0.0 copy-done.1
  3.7 0.0 copy-done.2
  3.7 0.0 copy-done.3
  3.7 45.1 %shard_map.68 = (bf16[16,64,256]{2,1,0:T(8,128)(2,1)S(1)}, bf16[16,64,256]{2,1,0:T(8,128)(2,1)S(1)}) custom-call(bf16[2,128,32,128]{3,2,1,0:T(8,128)(2,1)S(1)} %bitcast.7, bf16[3,3,3,32,256]{4,3,2,1,0:T(8,128)(2,1)S(1)} %copy-done, f32[1,256]{1,0:T(1,128)S(1)} %bitcast.10, bf16[3,3,3,32,256]{4,3,2,1,0:T(8,128)(2,1)S(1)} %copy-done.1, f32[1,256]{1,0:T(1,128)S(1)} %bitcast.11), custom_call_target="tpu_custom_call" | custom-call | tf_op jit(solution)/shard_map/pallas_call | solution.py:250
  48.8 0.8 %copy.12 = bf16[1,16,64,256]{3,2,1,0:T(8,128)(2,1)} copy(bf16[1,16,64,256]{3,2,1,0:T(8,128)(2,1)S(1)} %bitcast.9) | data formatting | bytes 1048576
  49.6 0.8 %copy.13 = bf16[1,16,64,256]{3,2,1,0:T(8,128)(2,1)} copy(bf16[1,16,64,256]{3,2,1,0:T(8,128)(2,1)S(1)} %bitcast.8) | data formatting | bytes 1048576
Async XLA Ops:
  0.6 3.1 %copy-start = (bf16[3,3,3,32,256]{4,3,2,1,0:T(8,128)(2,1)S(1)}, bf16[3,3,3,32,256]{4,3,2,1,0:T(8,128)(2,1)}, u32[]{:S(2)}) copy-start(bf16[3,3,3,32,256]{4,3,2,1,0:T(8,128)(2,1)} %k1_ref.1) | copy-start | bytes 1327108
  0.6 3.1 %copy-start.1 = (bf16[3,3,3,32,256]{4,3,2,1,0:T(8,128)(2,1)S(1)}, bf16[3,3,3,32,256]{4,3,2,1,0:T(8,128)(2,1)}, u32[]{:S(2)}) copy-start(bf16[3,3,3,32,256]{4,3,2,1,0:T(8,128)(2,1)} %k2_ref.1) | copy-start | bytes 1327108
  0.7 3.1 %copy-start.2 = (f32[256]{0:T(256)S(1)}, f32[256]{0:T(256)}, u32[]{:S(2)}) copy-start(f32[256]{0:T(256)} %param.7) | copy-start | bytes 3076
  0.7 3.1 %copy-start.3 = (f32[256]{0:T(256)S(1)}, f32[256]{0:T(256)}, u32[]{:S(2)}) copy-start(f32[256]{0:T(256)} %param.9) | copy-start | bytes 3076

commit v3 on v2

--- a/solution.py
+++ b/solution.py
@@ -129,7 +129,42 @@
             send_sem=sum_send.at[s - 1, h], recv_sem=sum_recv.at[s - 1, h],
             device_id={"chan": to, "slab": slab}, device_id_type=MESH)
 
-    if step == 4 * outs:
+    paired = parts == 4 and step == 4 * outs
+    hop = step // 2
+
+    def stage(slot, h, u):
+        to = peer(jnp.int32(1 + u if slot < 2 else 2 - u))
+        block = peer(jnp.int32(3)) if slot == 1 else to
+        at = h * step + u * hop
+        return pltpu.make_async_remote_copy(
+            src_ref=part_ref.at[pl.ds(block * mine + at, hop)], dst_ref=recv_ref.at[slot, pl.ds(at, hop)],
+            send_sem=sum_send.at[slot, 2 * h + u], recv_sem=sum_recv.at[slot, 2 * h + u],
+            device_id={"chan": to, "slab": slab}, device_id_type=MESH)
+
+    if paired:
+        far, across_x, across_y = (peer(jnp.int32(s)) for s in (3, 1, 2))
+
+        def first(h, carry):
+            chunk(far * pieces + h)
+            stage(1, h, 0).start()
+            stage(1, h, 1).start()
+            chunk(across_x * pieces + h)
+            stage(0, h, 0).start()
+            chunk(across_y * pieces + h)
+            stage(0, h, 1).start()
+            return carry
+
+        lax.fori_loop(0, pieces, first, 0)
+        for h in range(pieces):
+            for u, block in ((0, across_y), (1, across_x)):
+                at = h * step + u * hop
+                stage(1, h, u).wait_recv()
+                here = pl.ds(block * mine + at, hop)
+                both = part_ref[here].astype(F32) + recv_ref[1, at:at + hop].astype(F32)
+                part_ref[here] = both.astype(BF)
+                stage(2, h, u).start()
+            chunk(me * pieces + h)
+    elif step == 4 * outs:
         def away(n, carry):
             s, h = parts - 1 - lax.rem(n, parts - 1), lax.div(n, parts - 1)
             chunk(peer(s) * pieces + h)
@@ -181,12 +216,15 @@
                 dst[...] = jnp.zeros(dst.shape, BF)
 
     for h in range(pieces):
-        for s in range(1, parts):
+        for slot in (0, 2) if paired else ():
+            stage(slot, h, 0).wait_recv()
+            stage(slot, h, 1).wait_recv()
+        for s in () if paired else range(1, parts):
             sum_copy(jnp.int32(s), h).wait_recv()
         for r in range(h * step, (h + 1) * step, 4):
             total = part_ref[pl.ds(me * mine + r, 4)].astype(F32)
-            for s in range(1, parts):
-                total += recv_ref[s - 1, r:r + 4].astype(F32)
+            for slot in (0, 2) if paired else range(parts - 1):
+                total += recv_ref[slot, r:r + 4].astype(F32)
             act = leaky(total + b1_ref[...]).astype(BF)
             act_ref[r:r + 4] = act
             a_ref[1, r + 1:r + 5] = act
@@ -228,7 +266,11 @@
         low_copy().wait_send()
     for s in range(1, parts):
         for h in range(pieces):
-            sum_copy(jnp.int32(s), h).wait_send()
+            if paired:
+                stage(s - 1, h, 0).wait_send()
+                stage(s - 1, h, 1).wait_send()
+            else:
+                sum_copy(jnp.int32(s), h).wait_send()
     for n, (dc, ds) in enumerate(AROUND):
         for h in due(dc):
             @pl.when(inside(dc, ds))
@@ -262,7 +304,7 @@
             pltpu.VMEM((3, 3, 3 * k, k), BF),
             pltpu.VMEM((3, mine * cols, k), F32),
             dma, dma,
-            dma((parts - 1, mine // step)), dma((parts - 1, mine // step)),
+            dma((parts - 1, 2 * mine // step)), dma((parts - 1, 2 * mine // step)),
             dma((8, mine // step)), dma((8, mine // step)),
         ],
         compiler_params=pltpu.CompilerParams(vmem_limit_bytes=48 << 20, collective_id=0, has_side_effects=True),

time: 50.8 us -> 46.4 us (0.913)
  Pallas kernels: 45.1 us -> 40.7 us
    pallas_call x1, Pallas kernels: 45.1 us -> 40.7 us  [local(): pl.pallas_call(functools.partial(body, parts, slabs), out_shape=(block, b...]
where the time goes in v3:
time: 46.4 us; the launch traced here: 46 us
  Pallas kernels  40.7 us (88%)
  local copies, waits for them, and re-layouts  4.62 us (10%)
  between operations  0.7 us (2%)
    pallas_call x1, Pallas kernels, local(): pl.pallas_call(functools.partial(body, parts, slabs), out_shape=(block, b...  40.7 us
    unnamed x11, local copies, waits for them, and re-layouts  4.62 us

profile of v3, /device:TPU:1, one launch (start us, length us, event | category | flops | bytes accessed | tf_op | source)
XLA Modules:
  0.0 46.0 jit_solution(9569670916853000534)
XLA Ops:
  0.6 0.0 copy-start
  0.6 0.0 copy-start.1
  0.7 0.0 copy-start.2
  0.7 0.0 copy-start.3
  0.7 3.0 %copy.9 = bf16[32,2,128,128]{3,0,2,1:T(8,128)(2,1)S(1)} copy(bf16[32,2,128,128]{3,2,1,0:T(8,128)(2,1)} %param.5) | data formatting | bytes 4194304 | tf_op args[0]
  3.7 0.0 copy-done
  3.7 0.0 copy-done.1
  3.7 0.0 copy-done.2
  3.7 0.0 copy-done.3
  3.7 40.7 %shard_map.68 = (bf16[16,64,256]{2,1,0:T(8,128)(2,1)S(1)}, bf16[16,64,256]{2,1,0:T(8,128)(2,1)S(1)}) custom-call(bf16[2,128,32,128]{3,2,1,0:T(8,128)(2,1)S(1)} %bitcast.7, bf16[3,3,3,32,256]{4,3,2,1,0:T(8,128)(2,1)S(1)} %copy-done, f32[1,256]{1,0:T(1,128)S(1)} %bitcast.10, bf16[3,3,3,32,256]{4,3,2,1,0:T(8,128)(2,1)S(1)} %copy-done.1, f32[1,256]{1,0:T(1,128)S(1)} %bitcast.11), custom_call_target="tpu_custom_call" | custom-call | tf_op jit(solution)/shard_map/pallas_call | solution.py:292
  44.5 0.8 %copy.12 = bf16[1,16,64,256]{3,2,1,0:T(8,128)(2,1)} copy(bf16[1,16,64,256]{3,2,1,0:T(8,128)(2,1)S(1)} %bitcast.9) | data formatting | bytes 1048576
  45.3 0.8 %copy.13 = bf16[1,16,64,256]{3,2,1,0:T(8,128)(2,1)} copy(bf16[1,16,64,256]{3,2,1,0:T(8,128)(2,1)S(1)} %bitcast.8) | data formatting | bytes 1048576
Async XLA Ops:
  0.6 3.1 %copy-start = (bf16[3,3,3,32,256]{4,3,2,1,0:T(8,128)(2,1)S(1)}, bf16[3,3,3,32,256]{4,3,2,1,0:T(8,128)(2,1)}, u32[]{:S(2)}) copy-start(bf16[3,3,3,32,256]{4,3,2,1,0:T(8,128)(2,1)} %k1_ref.1) | copy-start | bytes 1327108
  0.6 3.1 %copy-start.1 = (bf16[3,3,3,32,256]{4,3,2,1,0:T(8,128)(2,1)S(1)}, bf16[3,3,3,32,256]{4,3,2,1,0:T(8,128)(2,1)}, u32[]{:S(2)}) copy-start(bf16[3,3,3,32,256]{4,3,2,1,0:T(8,128)(2,1)} %k2_ref.1) | copy-start | bytes 1327108
  0.7 3.1 %copy-start.2 = (f32[256]{0:T(256)S(1)}, f32[256]{0:T(256)}, u32[]{:S(2)}) copy-start(f32[256]{0:T(256)} %param.7) | copy-start | bytes 3076
  0.7 3.1 %copy-start.3 = (f32[256]{0:T(256)S(1)}, f32[256]{0:T(256)}, u32[]{:S(2)}) copy-start(f32[256]{0:T(256)} %param.9) | copy-start | bytes 3076
